TPU v7x, 32 devices: a whole 2x2x4 slice. The times are simulated.
32 devices in a mesh: range: 8 (over z, y), alt: 4 (over x, core), freq: 1.
Axes of the slice: x: 2, y: 2, z: 4, core: 2. Of those that a mesh axis runs over, the one named last changes fastest.
Arguments:
- freq_scale: float32 [2], P('freq'), may hold values from 1 to 2
- base_profile: float32 [1024], P('alt'), may hold values from 1.5 to 3
- perturb: float32 [32, 1024], P('range', 'alt'), may hold values from -1 to 1
- start_block: float32 [96, 1024], P(None, 'alt'), may hold values from -6 to 6
- source: float32 [2, 2, 96], P('freq'), may hold values from -6 to 6
Outputs:
- field: float32 [2, 32, 2, 1024], P('freq', 'range', None, 'alt')
All inputs are finite; a program needn't handle non-finite values.
Results may differ from a plain program's by a relative error of at most 0.0003.
Values sent between devices are 32-bit elements; how exact they have to be, the bound alone decides.
No kernel may reach another device: no remote copies, remote signals or barrier semaphores. Data moves between devices by JAX's collectives and lax.ppermute only.
A program may use at most 128 MiB of HBM per device.

v0:
```python
import jax
import jax.numpy as jnp
from jax import lax
from jax.sharding import PartitionSpec as P

ITERS = 8
phase_step = 0.15
relief = 0.1


def with_halo(block, sides, width):
    for axis, dim in sides:
        count = lax.axis_size(axis)
        forward = [(i, i + 1) for i in range(count - 1)]
        backward = [(target, source) for source, target in forward]
        low = lax.ppermute(
            lax.slice_in_dim(block, block.shape[dim] - width, None, axis=dim), axis, forward
        )
        high = lax.ppermute(lax.slice_in_dim(block, 0, width, axis=dim), axis, backward)
        block = jnp.concatenate([low, block, high], axis=dim)
    return block


def shifted(value, axis, steps):
    count = lax.axis_size(axis)
    first, last = (max(0, -steps), min(count, count - steps))
    return lax.ppermute(value, axis, [(source, source + steps) for source in range(first, last)])


def mult(left, right):
    return jnp.einsum("...ij,...jk->...ik", left, right, precision=lax.Precision.HIGHEST)


def inner(left, right):
    return jnp.einsum("...mz,...nz->...mn", left, right, precision=lax.Precision.HIGHEST)


def solve_lower(lower, values):
    return lax.linalg.triangular_solve(lower, values, left_side=True, lower=True)


def build_transfer(ritz, correlation):
    count = ritz.shape[-1]
    unit = jnp.eye(count, dtype=ritz.dtype)
    phase = phase_step * ritz
    square = mult(phase, phase)
    cosine = unit - 0.5 * square + mult(square, square) / 24.0
    sine = phase - mult(phase, square) / 6.0
    turned = mult(correlation, cosine)
    skewed = mult(correlation, sine)
    upper = jnp.concatenate([turned, -skewed], axis=-1)
    below = jnp.concatenate([skewed, turned], axis=-1)
    return jnp.concatenate([upper, below], axis=-2)


def local(freq_scale, base_profile, perturb, start_block, source):
    freqs = freq_scale.shape[0]
    seg_count = perturb.shape[0]
    modes = start_block.shape[0]
    alt_local = start_block.shape[1]
    alt_total = alt_local * lax.axis_size("alt")
    coef = (
        freq_scale[:, None, None, None]
        * (base_profile[None, :] * (1.0 + relief * perturb))[None, :, None, :]
    )

    def apply_operator(block):
        padded = with_halo(block, (("alt", 3),), 1)
        return coef * block + 0.5 * (padded[..., 2:] + padded[..., :-2])

    iter_count = ITERS
    basis = jnp.broadcast_to(
        start_block / jnp.sqrt(float(alt_total)), (freqs, seg_count) + start_block.shape
    )
    for step in range(iter_count):
        image = apply_operator(basis)
        gram = lax.psum(inner(image, image), "alt")
        basis = solve_lower(jnp.linalg.cholesky(gram), image)
    himage = apply_operator(basis)
    upcoming = shifted(basis[:, 0], "range", -1)
    ahead = jnp.concatenate([basis[:, 1:], upcoming[:, None]], axis=1)
    ritz, correlation = lax.psum((inner(basis, himage), inner(ahead, basis)), "alt")
    transfer = build_transfer(ritz, correlation)
    width = 2 * modes
    product = jnp.broadcast_to(jnp.eye(width, dtype=jnp.float32), (freqs, width, width))
    for seg in range(seg_count):
        product = mult(transfer[:, seg], product)
    start = jnp.concatenate([source[:, 0], source[:, 1]], axis=-1)
    position = lax.axis_index("range")
    carry = jnp.where(position == 0, start, jnp.zeros_like(start))

    def relay_step(turn, state):
        leaving = jnp.einsum("fij,fj->fi", product, state, precision=lax.Precision.HIGHEST)
        arrived = shifted(leaving, "range", 1)
        return jnp.where(position == turn + 1, arrived, state)

    carry = lax.fori_loop(0, lax.axis_size("range") - 1, relay_step, carry)
    amp_list = []
    state = carry
    for seg in range(seg_count):
        amp_list.append(state)
        if seg + 1 < seg_count:
            state = jnp.einsum(
                "fij,fj->fi", transfer[:, seg], state, precision=lax.Precision.HIGHEST
            )
    amps = jnp.stack(amp_list, axis=1).reshape(freqs, seg_count, 2, modes)
    scale = jnp.sqrt(float(alt_total) / float(modes))
    return scale * jnp.einsum("fspm,fsmz->fspz", amps, basis, precision=lax.Precision.HIGHEST)


def solution(mesh):
    in_specs = (P("freq"), P("alt"), P("range", "alt"), P(None, "alt"), P("freq", None, None))
    out_specs = P("freq", "range", None, "alt")
    return jax.shard_map(local, mesh=mesh, in_specs=in_specs, out_specs=out_specs, check_vma=False)
```

profile of v0, /device:TPU:8, one launch (start us, length us, event | category | flops | bytes accessed | tf_op | source)
XLA Modules:
  0.0 1563.9 jit_solution(673033635187756319)
XLA Ops:
  16.3 39.1 %all-reduce.11.cloned.1.call-done = f32[2,4,96,96]{2,3,1,0:T(8,128)} async-done(((f32[2,4,96,96]{2,3,1,0:T(8,128)}), f32[2,4,96,96]{2,3,1,0:T(8,128)}) %all-reduce.11.cloned.1.call-update) | async-done | bytes 294928 | tf_op jit(solution)/shard_map/psum | solution.py:77
  57.6 70.3 %custom-call.20 = f32[2,4,96,96]{3,2,1,0:T(8,128)S(1)} custom-call(f32[2,4,96,96]{3,2,1,0:T(8,128)S(1)} %fusion.64), custom_call_target="Cholesky" | custom-call | tf_op jit(solution)/shard_map/jit(cholesky)/cholesky | solution.py:78
  128.3 59.0 %custom-call.21 = f32[2,4,1,96,96]{3,4,2,1,0:T(8,128)S(1)} custom-call(f32[2,4,1,96,96]{4,3,2,1,0:T(8,128)S(1)} %select_bitcast_fusion.7), custom_call_target="InvertDiagBlocksLowerTriangular" | custom-call | tf_op jit(solution)/shard_map/triangular_solve/custom-call.0 | solution.py:39
  197.4 37.7 %all-reduce.13.cloned.1.call-done = f32[2,4,96,96]{2,3,1,0:T(8,128)} async-done(((f32[2,4,96,96]{2,3,1,0:T(8,128)}), f32[2,4,96,96]{2,3,1,0:T(8,128)}) %all-reduce.13.cloned.1.call-update) | async-done | bytes 294928 | tf_op jit(solution)/shard_map/psum | solution.py:77
  237.3 70.3 %custom-call.22 = f32[2,4,96,96]{3,2,1,0:T(8,128)S(1)} custom-call(f32[2,4,96,96]{3,2,1,0:T(8,128)S(1)} %fusion.61), custom_call_target="Cholesky" | custom-call | tf_op jit(solution)/shard_map/jit(cholesky)/cholesky | solution.py:78
  308.0 59.0 %custom-call.23 = f32[2,4,1,96,96]{3,4,2,1,0:T(8,128)S(1)} custom-call(f32[2,4,1,96,96]{4,3,2,1,0:T(8,128)S(1)} %select_bitcast_fusion.6), custom_call_target="InvertDiagBlocksLowerTriangular" | custom-call | tf_op jit(solution)/shard_map/triangular_solve/custom-call.0 | solution.py:39
  377.4 37.5 %all-reduce.15.cloned.1.call-done = f32[2,4,96,96]{2,3,1,0:T(8,128)} async-done(((f32[2,4,96,96]{2,3,1,0:T(8,128)}), f32[2,4,96,96]{2,3,1,0:T(8,128)}) %all-reduce.15.cloned.1.call-update) | async-done | bytes 294928 | tf_op jit(solution)/shard_map/psum | solution.py:77
  417.0 70.3 %custom-call.24 = f32[2,4,96,96]{3,2,1,0:T(8,128)S(1)} custom-call(f32[2,4,96,96]{3,2,1,0:T(8,128)S(1)} %fusion.58), custom_call_target="Cholesky" | custom-call | tf_op jit(solution)/shard_map/jit(cholesky)/cholesky | solution.py:78
  487.7 59.0 %custom-call.25 = f32[2,4,1,96,96]{3,4,2,1,0:T(8,128)S(1)} custom-call(f32[2,4,1,96,96]{4,3,2,1,0:T(8,128)S(1)} %select_bitcast_fusion.5), custom_call_target="InvertDiagBlocksLowerTriangular" | custom-call | tf_op jit(solution)/shard_map/triangular_solve/custom-call.0 | solution.py:39
  556.7 37.8 %all-reduce.17.cloned.1.call-done = f32[2,4,96,96]{2,3,1,0:T(8,128)} async-done(((f32[2,4,96,96]{2,3,1,0:T(8,128)}), f32[2,4,96,96]{2,3,1,0:T(8,128)}) %all-reduce.17.cloned.1.call-update) | async-done | bytes 294928 | tf_op jit(solution)/shard_map/psum | solution.py:77
  596.8 70.3 %custom-call.26 = f32[2,4,96,96]{3,2,1,0:T(8,128)S(1)} custom-call(f32[2,4,96,96]{3,2,1,0:T(8,128)S(1)} %fusion.55), custom_call_target="Cholesky" | custom-call | tf_op jit(solution)/shard_map/jit(cholesky)/cholesky | solution.py:78
  667.5 59.0 %custom-call.27 = f32[2,4,1,96,96]{3,4,2,1,0:T(8,128)S(1)} custom-call(f32[2,4,1,96,96]{4,3,2,1,0:T(8,128)S(1)} %select_bitcast_fusion.4), custom_call_target="InvertDiagBlocksLowerTriangular" | custom-call | tf_op jit(solution)/shard_map/triangular_solve/custom-call.0 | solution.py:39
  736.5 38.1 %all-reduce.19.cloned.1.call-done = f32[2,4,96,96]{2,3,1,0:T(8,128)} async-done(((f32[2,4,96,96]{2,3,1,0:T(8,128)}), f32[2,4,96,96]{2,3,1,0:T(8,128)}) %all-reduce.19.cloned.1.call-update) | async-done | bytes 294928 | tf_op jit(solution)/shard_map/psum | solution.py:77
  776.8 70.3 %custom-call.28 = f32[2,4,96,96]{3,2,1,0:T(8,128)S(1)} custom-call(f32[2,4,96,96]{3,2,1,0:T(8,128)S(1)} %fusion.52), custom_call_target="Cholesky" | custom-call | tf_op jit(solution)/shard_map/jit(cholesky)/cholesky | solution.py:78
  847.5 59.0 %custom-call.29 = f32[2,4,1,96,96]{3,4,2,1,0:T(8,128)S(1)} custom-call(f32[2,4,1,96,96]{4,3,2,1,0:T(8,128)S(1)} %select_bitcast_fusion.3), custom_call_target="InvertDiagBlocksLowerTriangular" | custom-call | tf_op jit(solution)/shard_map/triangular_solve/custom-call.0 | solution.py:39
  916.6 37.8 %all-reduce.21.cloned.1.call-done = f32[2,4,96,96]{2,3,1,0:T(8,128)} async-done(((f32[2,4,96,96]{2,3,1,0:T(8,128)}), f32[2,4,96,96]{2,3,1,0:T(8,128)}) %all-reduce.21.cloned.1.call-update) | async-done | bytes 294928 | tf_op jit(solution)/shard_map/psum | solution.py:77
  956.5 70.3 %custom-call.30 = f32[2,4,96,96]{3,2,1,0:T(8,128)S(1)} custom-call(f32[2,4,96,96]{3,2,1,0:T(8,128)S(1)} %fusion.49), custom_call_target="Cholesky" | custom-call | tf_op jit(solution)/shard_map/jit(cholesky)/cholesky | solution.py:78
  1027.2 59.0 %custom-call.31 = f32[2,4,1,96,96]{3,4,2,1,0:T(8,128)S(1)} custom-call(f32[2,4,1,96,96]{4,3,2,1,0:T(8,128)S(1)} %select_bitcast_fusion.2), custom_call_target="InvertDiagBlocksLowerTriangular" | custom-call | tf_op jit(solution)/shard_map/triangular_solve/custom-call.0 | solution.py:39
  1096.4 37.7 %all-reduce.23.cloned.1.call-done = f32[2,4,96,96]{2,3,1,0:T(8,128)} async-done(((f32[2,4,96,96]{2,3,1,0:T(8,128)}), f32[2,4,96,96]{2,3,1,0:T(8,128)}) %all-reduce.23.cloned.1.call-update) | async-done | bytes 294928 | tf_op jit(solution)/shard_map/psum | solution.py:77
  1136.3 70.3 %custom-call.32 = f32[2,4,96,96]{3,2,1,0:T(8,128)S(1)} custom-call(f32[2,4,96,96]{3,2,1,0:T(8,128)S(1)} %fusion.46), custom_call_target="Cholesky" | custom-call | tf_op jit(solution)/shard_map/jit(cholesky)/cholesky | solution.py:78
  1206.9 59.0 %custom-call.33 = f32[2,4,1,96,96]{3,4,2,1,0:T(8,128)S(1)} custom-call(f32[2,4,1,96,96]{4,3,2,1,0:T(8,128)S(1)} %select_bitcast_fusion.1), custom_call_target="InvertDiagBlocksLowerTriangular" | custom-call | tf_op jit(solution)/shard_map/triangular_solve/custom-call.0 | solution.py:39
  1316.0 70.3 %custom-call.34 = f32[2,4,96,96]{3,2,1,0:T(8,128)S(1)} custom-call(f32[2,4,96,96]{3,2,1,0:T(8,128)S(1)} %fusion.43), custom_call_target="Cholesky" | custom-call | tf_op jit(solution)/shard_map/jit(cholesky)/cholesky | solution.py:78
  1386.7 59.0 %custom-call.35 = f32[2,4,1,96,96]{3,4,2,1,0:T(8,128)S(1)} custom-call(f32[2,4,1,96,96]{4,3,2,1,0:T(8,128)S(1)} %select_bitcast_fusion), custom_call_target="InvertDiagBlocksLowerTriangular" | custom-call | tf_op jit(solution)/shard_map/triangular_solve/custom-call.0 | solution.py:39
  1506.9 47.9 %while.13 = (s32[]{:T(128)}, f32[2,192]{1,0:T(2,128)S(1)}, s32[]{:T(128)}, f32[2,192,192]{2,1,0:T(8,128)S(1)}, s32[]{:T(128)}) while((s32[]{:T(128)}, f32[2,192]{1,0:T(2,128)S(1)}, s32[]{:T(128)}, f32[2,192,192]{2,1,0:T(8,128)S(1)}, s32[]{:T(128)}) %tuple.45), condition=%wide.region_13.16_spmd, body=%wide.region_12.15_spmd.sunk | while | flops 885123 | bytes 311919 | solution.py:97
  (199 shorter events, 249.1 us)
Async XLA Ops:
  6.5 48.8 %all-reduce.11.cloned.1.call-start = ((), (), s32[]{:S(2)}) async-start(), calls=%async_computation | async-start | bytes 786432 | tf_op jit(solution)/shard_map/psum | solution.py:77
  7.7 5.9 collective-permute-start.1
  9.1 4.5 collective-permute-start.2
  16.2 218.9 %all-reduce.13.cloned.1.call-start = ((), (), s32[]{:S(2)}) async-start(), calls=%async_computation.1 | async-start | bytes 786432 | tf_op jit(solution)/shard_map/psum | solution.py:77
  190.2 4.4 collective-permute-start.4
  197.0 217.8 %all-reduce.15.cloned.1.call-start = ((), (), s32[]{:S(2)}) async-start(), calls=%async_computation.2 | async-start | bytes 786432 | tf_op jit(solution)/shard_map/psum | solution.py:77
  369.9 4.4 collective-permute-start.6
  376.8 217.8 %all-reduce.17.cloned.1.call-start = ((), (), s32[]{:S(2)}) async-start(), calls=%async_computation.3 | async-start | bytes 786432 | tf_op jit(solution)/shard_map/psum | solution.py:77
  556.5 218.1 %all-reduce.19.cloned.1.call-start = ((), (), s32[]{:S(2)}) async-start(), calls=%async_computation.4 | async-start | bytes 786432 | tf_op jit(solution)/shard_map/psum | solution.py:77
  736.2 218.1 %all-reduce.21.cloned.1.call-start = ((), (), s32[]{:S(2)}) async-start(), calls=%async_computation.5 | async-start | bytes 786432 | tf_op jit(solution)/shard_map/psum | solution.py:77
  916.3 217.8 %all-reduce.23.cloned.1.call-start = ((), (), s32[]{:S(2)}) async-start(), calls=%async_computation.6 | async-start | bytes 786432 | tf_op jit(solution)/shard_map/psum | solution.py:77
  1096.0 217.8 %all-reduce.25.cloned.1.call-start = ((), (), s32[]{:S(2)}) async-start(), calls=%async_computation.7 | async-start | bytes 786432 | tf_op jit(solution)/shard_map/psum | solution.py:77
  1267.6 4.4 collective-permute-start.15
  1275.7 221.3 %all-reduce.27.cloned.1.call-start = ((), (), s32[]{:S(2)}) async-start(), calls=%async_computation.8 | async-start | bytes 1572864 | tf_op jit(solution)/shard_map/psum | solution.py:82
  1447.3 8.0 collective-permute-start.18
  1448.6 6.7 collective-permute-start.19
  1451.7 8.8 collective-permute-start.17
  1507.4 6.4 collective-permute-start
  1514.2 6.4 collective-permute-start
  1521.0 6.4 collective-permute-start
  1527.9 6.4 collective-permute-start
  1534.7 6.4 collective-permute-start
  1541.5 6.4 collective-permute-start
  1548.4 6.4 collective-permute-start
  (13 other events, 59.0 us)
Sparse Core Ops, SparseCore 0:
  16.3 38.9 all-reduce.10
  197.2 37.8 all-reduce.12
  376.9 37.8 all-reduce.14
  556.6 37.8 all-reduce.16
  736.3 38.2 all-reduce.18
  916.4 37.8 all-reduce.20
  1096.1 37.8 all-reduce.22
  1275.9 37.8 all-reduce.24
  1462.3 34.6 all-reduce.26
where the time goes:
time: 1570 us; the launch traced here: 1560 us
  other arithmetic  1050 us (67%)
  waiting for transfers between devices  381 us (24%)
  starting transfers between devices  59 us (4%)
  matrix products  49.2 us (3%)
    another operation x25, other arithmetic, local(): basis = solve_lower(jnp.linalg.cholesky(gram), image)  564 us
    another operation x17, other arithmetic, solve_lower(): lax.linalg.triangular_solve(lower, values, left_side=True, lower=True)  473 us
    psum x8, waiting for transfers between devices, local(): gram = lax.psum(inner(image, image), 'alt')  303 us
    psum x1, waiting for transfers between devices, local(): lax.psum((inner(basis, himage), inner(ahead, basis)), 'alt')  34.7 us
    ppermute x8, waiting for transfers between devices, shifted(): lax.ppermute(value, axis, [(source, source + steps) for source in range(f...  32.3 us
  transfers between devices with their start and end apart: 35, of which 24 were waited for; matrix products, arithmetic and copies ran while one was open for 0% of the time, Pallas kernels for 0%

commit v1 on v0

--- a/solution.py
+++ b/solution.py
@@ -74,7 +74,8 @@
     )
     for step in range(iter_count):
         image = apply_operator(basis)
-        gram = lax.psum(inner(image, image), "alt")
+        u_in = inner(image, image)
+        gram = jnp.sum(lax.all_gather(u_in, "alt"), 0)
         basis = solve_lower(jnp.linalg.cholesky(gram), image)
     himage = apply_operator(basis)
     upcoming = shifted(basis[:, 0], "range", -1)

time: 1570 us -> 1470 us (0.936)
  waiting for transfers between devices: 381 us -> 286 us
    psum x8 -> x0, waiting for transfers between devices: 303 us -> none  [local(): gram = lax.psum(inner(image, image), 'alt')]
    all_gather x0 -> x8, waiting for transfers between devices: none -> 208 us  [local(): gram = jnp.sum(lax.all_gather(u_in, 'alt'), 0)]
where the time goes in v1:
time: 1470 us
  other arithmetic  1050 us (71%)
  waiting for transfers between devices  286 us (19%)
  starting transfers between devices  59.8 us (4%)
  matrix products  49.4 us (3%)
    another operation x25, other arithmetic, local(): basis = solve_lower(jnp.linalg.cholesky(gram), image)  564 us
    another operation x17, other arithmetic, solve_lower(): lax.linalg.triangular_solve(lower, values, left_side=True, lower=True)  473 us
    all_gather x8, waiting for transfers between devices, local(): gram = jnp.sum(lax.all_gather(u_in, 'alt'), 0)  208 us
    psum x1, waiting for transfers between devices, local(): lax.psum((inner(basis, himage), inner(ahead, basis)), 'alt')  35.4 us
    ppermute x8, waiting for transfers between devices, shifted(): lax.ppermute(value, axis, [(source, source + steps) for source in range(f...  32.6 us
  transfers between devices with their start and end apart: 35, of which 24 were waited for; matrix products, arithmetic and copies ran while one was open for 0% of the time, Pallas kernels for 0%

profile of v1, /device:TPU:8, one launch (start us, length us, event | category | flops | bytes accessed | tf_op | source)
XLA Modules:
  0.0 1466.7 jit_solution(5362007830544784050)
XLA Ops:
  16.3 26.1 %all-gather.17.cloned.1.call-done = f32[8,4,96,96]{3,2,1,0:T(8,128)} async-done(((f32[2,4,96,96]{3,2,1,0:T(8,128)}), f32[8,4,96,96]{3,2,1,0:T(8,128)}) %all-gather.17.cloned.1.call-update) | async-done | bytes 1179664 | tf_op jit(solution)/shard_map/all_gather | solution.py:78
  44.2 70.3 %custom-call.20 = f32[2,4,96,96]{3,2,1,0:T(8,128)S(1)} custom-call(f32[2,4,96,96]{3,2,1,0:T(8,128)S(1)} %fusion.64), custom_call_target="Cholesky" | custom-call | tf_op jit(solution)/shard_map/jit(cholesky)/cholesky | solution.py:79
  114.9 59.0 %custom-call.21 = f32[2,4,1,96,96]{3,4,2,1,0:T(8,128)S(1)} custom-call(f32[2,4,1,96,96]{4,3,2,1,0:T(8,128)S(1)} %select_bitcast_fusion.7), custom_call_target="InvertDiagBlocksLowerTriangular" | custom-call | tf_op jit(solution)/shard_map/triangular_solve/custom-call.0 | solution.py:39
  184.1 26.1 %all-gather.19.cloned.1.call-done = f32[8,4,96,96]{3,2,1,0:T(8,128)} async-done(((f32[2,4,96,96]{3,2,1,0:T(8,128)}), f32[8,4,96,96]{3,2,1,0:T(8,128)}) %all-gather.19.cloned.1.call-update) | async-done | bytes 1179664 | tf_op jit(solution)/shard_map/all_gather | solution.py:78
  212.0 70.3 %custom-call.22 = f32[2,4,96,96]{3,2,1,0:T(8,128)S(1)} custom-call(f32[2,4,96,96]{3,2,1,0:T(8,128)S(1)} %fusion.61), custom_call_target="Cholesky" | custom-call | tf_op jit(solution)/shard_map/jit(cholesky)/cholesky | solution.py:79
  282.7 59.0 %custom-call.23 = f32[2,4,1,96,96]{3,4,2,1,0:T(8,128)S(1)} custom-call(f32[2,4,1,96,96]{4,3,2,1,0:T(8,128)S(1)} %select_bitcast_fusion.6), custom_call_target="InvertDiagBlocksLowerTriangular" | custom-call | tf_op jit(solution)/shard_map/triangular_solve/custom-call.0 | solution.py:39
  379.8 70.3 %custom-call.24 = f32[2,4,96,96]{3,2,1,0:T(8,128)S(1)} custom-call(f32[2,4,96,96]{3,2,1,0:T(8,128)S(1)} %fusion.58), custom_call_target="Cholesky" | custom-call | tf_op jit(solution)/shard_map/jit(cholesky)/cholesky | solution.py:79
  450.5 59.0 %custom-call.25 = f32[2,4,1,96,96]{3,4,2,1,0:T(8,128)S(1)} custom-call(f32[2,4,1,96,96]{4,3,2,1,0:T(8,128)S(1)} %select_bitcast_fusion.5), custom_call_target="InvertDiagBlocksLowerTriangular" | custom-call | tf_op jit(solution)/shard_map/triangular_solve/custom-call.0 | solution.py:39
  519.5 26.2 %all-gather.23.cloned.1.call-done = f32[8,4,96,96]{3,2,1,0:T(8,128)} async-done(((f32[2,4,96,96]{3,2,1,0:T(8,128)}), f32[8,4,96,96]{3,2,1,0:T(8,128)}) %all-gather.23.cloned.1.call-update) | async-done | bytes 1179664 | tf_op jit(solution)/shard_map/all_gather | solution.py:78
  547.5 70.3 %custom-call.26 = f32[2,4,96,96]{3,2,1,0:T(8,128)S(1)} custom-call(f32[2,4,96,96]{3,2,1,0:T(8,128)S(1)} %fusion.55), custom_call_target="Cholesky" | custom-call | tf_op jit(solution)/shard_map/jit(cholesky)/cholesky | solution.py:79
  618.2 59.0 %custom-call.27 = f32[2,4,1,96,96]{3,4,2,1,0:T(8,128)S(1)} custom-call(f32[2,4,1,96,96]{4,3,2,1,0:T(8,128)S(1)} %select_bitcast_fusion.4), custom_call_target="InvertDiagBlocksLowerTriangular" | custom-call | tf_op jit(solution)/shard_map/triangular_solve/custom-call.0 | solution.py:39
  714.3 70.3 %custom-call.28 = f32[2,4,96,96]{3,2,1,0:T(8,128)S(1)} custom-call(f32[2,4,96,96]{3,2,1,0:T(8,128)S(1)} %fusion.52), custom_call_target="Cholesky" | custom-call | tf_op jit(solution)/shard_map/jit(cholesky)/cholesky | solution.py:79
  785.0 59.0 %custom-call.29 = f32[2,4,1,96,96]{3,4,2,1,0:T(8,128)S(1)} custom-call(f32[2,4,1,96,96]{4,3,2,1,0:T(8,128)S(1)} %select_bitcast_fusion.3), custom_call_target="InvertDiagBlocksLowerTriangular" | custom-call | tf_op jit(solution)/shard_map/triangular_solve/custom-call.0 | solution.py:39
  854.1 26.2 %all-gather.27.cloned.1.call-done = f32[8,4,96,96]{3,2,1,0:T(8,128)} async-done(((f32[2,4,96,96]{3,2,1,0:T(8,128)}), f32[8,4,96,96]{3,2,1,0:T(8,128)}) %all-gather.27.cloned.1.call-update) | async-done | bytes 1179664 | tf_op jit(solution)/shard_map/all_gather | solution.py:78
  882.1 70.3 %custom-call.30 = f32[2,4,96,96]{3,2,1,0:T(8,128)S(1)} custom-call(f32[2,4,96,96]{3,2,1,0:T(8,128)S(1)} %fusion.49), custom_call_target="Cholesky" | custom-call | tf_op jit(solution)/shard_map/jit(cholesky)/cholesky | solution.py:79
  952.8 59.0 %custom-call.31 = f32[2,4,1,96,96]{3,4,2,1,0:T(8,128)S(1)} custom-call(f32[2,4,1,96,96]{4,3,2,1,0:T(8,128)S(1)} %select_bitcast_fusion.2), custom_call_target="InvertDiagBlocksLowerTriangular" | custom-call | tf_op jit(solution)/shard_map/triangular_solve/custom-call.0 | solution.py:39
  1022.1 25.9 %all-gather.29.cloned.1.call-done = f32[8,4,96,96]{3,2,1,0:T(8,128)} async-done(((f32[2,4,96,96]{3,2,1,0:T(8,128)}), f32[8,4,96,96]{3,2,1,0:T(8,128)}) %all-gather.29.cloned.1.call-update) | async-done | bytes 1179664 | tf_op jit(solution)/shard_map/all_gather | solution.py:78
  1049.9 70.3 %custom-call.32 = f32[2,4,96,96]{3,2,1,0:T(8,128)S(1)} custom-call(f32[2,4,96,96]{3,2,1,0:T(8,128)S(1)} %fusion.46), custom_call_target="Cholesky" | custom-call | tf_op jit(solution)/shard_map/jit(cholesky)/cholesky | solution.py:79
  1120.5 59.0 %custom-call.33 = f32[2,4,1,96,96]{3,4,2,1,0:T(8,128)S(1)} custom-call(f32[2,4,1,96,96]{4,3,2,1,0:T(8,128)S(1)} %select_bitcast_fusion.1), custom_call_target="InvertDiagBlocksLowerTriangular" | custom-call | tf_op jit(solution)/shard_map/triangular_solve/custom-call.0 | solution.py:39
  1189.6 26.2 %all-gather.31.cloned.1.call-done = f32[8,4,96,96]{3,2,1,0:T(8,128)} async-done(((f32[2,4,96,96]{3,2,1,0:T(8,128)}), f32[8,4,96,96]{3,2,1,0:T(8,128)}) %all-gather.31.cloned.1.call-update) | async-done | bytes 1179664 | tf_op jit(solution)/shard_map/all_gather | solution.py:78
  1217.6 70.3 %custom-call.34 = f32[2,4,96,96]{3,2,1,0:T(8,128)S(1)} custom-call(f32[2,4,96,96]{3,2,1,0:T(8,128)S(1)} %fusion.43), custom_call_target="Cholesky" | custom-call | tf_op jit(solution)/shard_map/jit(cholesky)/cholesky | solution.py:79
  1288.3 59.0 %custom-call.35 = f32[2,4,1,96,96]{3,4,2,1,0:T(8,128)S(1)} custom-call(f32[2,4,1,96,96]{4,3,2,1,0:T(8,128)S(1)} %select_bitcast_fusion), custom_call_target="InvertDiagBlocksLowerTriangular" | custom-call | tf_op jit(solution)/shard_map/triangular_solve/custom-call.0 | solution.py:39
  1364.4 35.4 %all-reduce.3.cloned.1.call-done = (f32[2,4,96,96]{3,2,1,0:T(8,128)}, f32[2,4,96,96]{3,2,1,0:T(8,128)}) async-done(((f32[2,4,96,96]{3,2,1,0:T(8,128)}, f32[2,4,96,96]{3,2,1,0:T(8,128)}), (f32[2,4,96,96]{3,2,1,0:T(8,128)}, f32[2,4,96,96]{3,2,1,0:T(8,128)})) %all-reduce.3.cloned.1.call-update) | async-done | bytes 589840 | tf_op jit(solution)/shard_map/psum | solution.py:83
  1409.7 47.9 %while.13 = (s32[]{:T(128)}, f32[2,192]{1,0:T(2,128)S(1)}, s32[]{:T(128)}, f32[2,192,192]{2,1,0:T(8,128)S(1)}, s32[]{:T(128)}) while((s32[]{:T(128)}, f32[2,192]{1,0:T(2,128)S(1)}, s32[]{:T(128)}, f32[2,192,192]{2,1,0:T(8,128)S(1)}, s32[]{:T(128)}) %tuple.45), condition=%wide.region_13.16_spmd, body=%wide.region_12.15_spmd.sunk | while | flops 885123 | bytes 311919 | solution.py:98
  (207 shorter events, 225.3 us)
Async XLA Ops:
  6.5 35.9 %all-gather.17.cloned.1.call-start = ((), (), s32[]{:S(2)}) async-start(), calls=%async_computation | async-start | bytes 1966080 | tf_op jit(solution)/shard_map/all_gather | solution.py:78
  7.7 5.9 collective-permute-start.1
  9.1 4.5 collective-permute-start.2
  16.2 194.0 %all-gather.19.cloned.1.call-start = ((), (), s32[]{:S(2)}) async-start(), calls=%async_computation.1 | async-start | bytes 1966080 | tf_op jit(solution)/shard_map/all_gather | solution.py:78
  176.8 4.4 collective-permute-start.4
  183.7 194.2 %all-gather.21.cloned.1.call-start = ((), (), s32[]{:S(2)}) async-start(), calls=%async_computation.2 | async-start | bytes 1966080 | tf_op jit(solution)/shard_map/all_gather | solution.py:78
  344.6 4.4 collective-permute-start.6
  351.5 194.2 %all-gather.23.cloned.1.call-start = ((), (), s32[]{:S(2)}) async-start(), calls=%async_computation.3 | async-start | bytes 1966080 | tf_op jit(solution)/shard_map/all_gather | solution.py:78
  512.4 4.4 collective-permute-start.8
  519.3 193.2 %all-gather.25.cloned.1.call-start = ((), (), s32[]{:S(2)}) async-start(), calls=%async_computation.4 | async-start | bytes 1966080 | tf_op jit(solution)/shard_map/all_gather | solution.py:78
  687.1 193.1 %all-gather.27.cloned.1.call-start = ((), (), s32[]{:S(2)}) async-start(), calls=%async_computation.5 | async-start | bytes 1966080 | tf_op jit(solution)/shard_map/all_gather | solution.py:78
  853.8 194.2 %all-gather.29.cloned.1.call-start = ((), (), s32[]{:S(2)}) async-start(), calls=%async_computation.6 | async-start | bytes 1966080 | tf_op jit(solution)/shard_map/all_gather | solution.py:78
  1021.6 194.2 %all-gather.31.cloned.1.call-start = ((), (), s32[]{:S(2)}) async-start(), calls=%async_computation.7 | async-start | bytes 1966080 | tf_op jit(solution)/shard_map/all_gather | solution.py:78
  1189.4 210.5 %all-reduce.3.cloned.1.call-start = ((), (), s32[]{:S(2)}) async-start(), calls=%async_computation.8 | async-start | bytes 1572864 | tf_op jit(solution)/shard_map/psum | solution.py:83
  1348.9 8.0 collective-permute-start.18
  1350.2 6.7 collective-permute-start.19
  1353.4 9.3 collective-permute-start.17
  1410.1 6.4 collective-permute-start
  1417.0 6.4 collective-permute-start
  1423.8 6.4 collective-permute-start
  1430.6 6.4 collective-permute-start
  1437.5 6.4 collective-permute-start
  1444.3 6.4 collective-permute-start
  1451.1 6.4 collective-permute-start
  (13 other events, 58.8 us)
Sparse Core Ops, SparseCore 0:
  16.3 26.0 all-gather.16
  183.8 26.2 all-gather.18
  351.6 26.2 all-gather.20
  519.4 26.2 all-gather.22
  687.3 25.1 all-gather.24
  853.9 26.2 all-gather.26
  1021.7 26.2 all-gather.28
  1189.5 26.2 all-gather.30
  1364.4 35.3 all-reduce.2
